TPU v7x, 32 devices: a whole 2x2x4 slice. The times are simulated.
32 devices in a mesh: row: 8 (over y, x, core), col: 4 (over z).
Axes of the slice: x: 2, y: 2, z: 4, core: 2. Of those that a mesh axis runs over, the one named last changes fastest.
Arguments:
- inverse_tiles: float32 [512, 512], P('row', 'col'), may hold values from -0.375 to 0.375
- factor_panels: float32 [3, 512, 256], P(None, 'row', 'col'), may hold values from -6 to 6
- block_rows: int32 [3, 8], replicated, may hold values from 0 to 15, as said below
- couplings: float32 [2, 512, 512], replicated, may hold values from -0.25 to 0.25
Outputs:
- new_columns: float32 [3, 512, 512], P(None, ('row', 'col'))
Inputs may be any that keep to these rules, and one draw needn't show every extreme that they name: `block_rows`: each row lists 8 different row blocks in no particular order; in each row, all 4 blocks q * 4 to q * 4 + 3 of some q are listed.
All inputs are finite; a program needn't handle non-finite values.
Results may differ from a plain program's by a relative error of at most 0.0001.
Values sent between devices are 32-bit elements; how exact they have to be, the bound alone decides.
No kernel may reach another device: no remote copies, remote signals or barrier semaphores. Data moves between devices by JAX's collectives and lax.ppermute only.
A program may use at most 64 MiB of HBM per device.

v0:
```python
import jax
import jax.numpy as jnp
from jax import lax
from jax.sharding import PartitionSpec as P


def on_device(inverse_tiles, factor_panels, block_rows, couplings):
    tile_rows, tile_cols = inverse_tiles.shape
    piece_rows = factor_panels.shape[1]
    listed = block_rows.shape[1]
    col_count = lax.axis_size("col")
    block_size = factor_panels.shape[2] * col_count // listed
    local_blocks = tile_cols // block_size
    my_column = lax.axis_index("col")
    offset = my_column * local_blocks
    targets = offset + jnp.arange(local_blocks, dtype=jnp.int32)
    results = []
    previous = None
    for section in range(factor_panels.shape[0]):
        section_rows = block_rows[section]
        gathered = lax.all_gather(factor_panels[section], "col", axis=1, tiled=True)
        onehot = (section_rows[:, None] == targets[None, :]).astype(jnp.float32)
        picked = jnp.einsum(
            "wpr,pq->wqr",
            gathered.reshape(piece_rows, listed, block_size),
            onehot,
            precision=lax.Precision.HIGHEST,
        ).reshape(piece_rows, tile_cols)
        partial_value = lax.dot_general(
            inverse_tiles,
            lax.all_gather(picked, "row", axis=0, tiled=True),
            (((1,), (1,)), ((), ())),
            precision=lax.Precision.HIGHEST,
            preferred_element_type=jnp.float32,
        )
        summed = lax.psum_scatter(partial_value, "col", scatter_dimension=0, tiled=True)
        if previous is not None:
            summed = summed + jnp.dot(
                previous,
                couplings[section - 1],
                precision=lax.Precision.HIGHEST,
                preferred_element_type=jnp.float32,
            )
        previous = -summed
        results.append(previous)
    return jnp.stack(results)


def solution(mesh):
    return jax.shard_map(
        on_device,
        mesh=mesh,
        in_specs=(P("row", "col"), P(None, "row", "col"), P(), P()),
        out_specs=P(None, ("row", "col"), None),
        check_vma=False,
    )
```

profile of v0, /device:TPU:0, one launch (start us, length us, event | category | flops | bytes accessed | tf_op | source)
XLA Modules:
  0.0 111.6 jit_solution(15987718816973304762)
XLA Ops:
  6.5 0.0 copy-start
  6.5 0.0 reduce-scatter.4.cloned.1.call-start
  6.5 0.8 fusion.23
  7.3 0.1 copy.26
  7.4 15.1 %all-gather = f32[1,64,256]{1,2,0:T(8,128)S(1)} all-gather(f32[1,64,64]{1,2,0:T(8,128)S(1)} %copy.26), channel_id=2, replica_groups=mesh['row'=8,'col'=4] {'col'}, dimensions={2}, use_global_device_ids=true | all-gather | bytes 81920 | tf_op jit(solution)/shard_map/all_gather | solution.py:21
  22.5 0.8 slice_bitcast_fusion.2
  23.3 0.3 convolution_bitcast_fusion.5
  23.6 0.0 copy-start.1
  23.6 0.1 copy.17
  23.7 9.4 %all_gather.19 = f32[512,128]{1,0:T(8,128)S(1)} all-gather(f32[64,128]{1,0:T(8,128)S(1)} %copy.17), channel_id=1, replica_groups=mesh['row'=8,'col'=4] {'row'}, dimensions={0}, use_global_device_ids=true | all-gather | bytes 294912 | tf_op jit(solution)/shard_map/all_gather | solution.py:31
  33.1 0.0 copy-done
  33.1 1.1 convolution_bitcast_fusion.2
  34.2 0.0 reduce-scatter.4.cloned.1.call-update
  34.2 0.0 reduce-scatter.6.cloned.1.call-start
  34.3 0.1 copy.27
  34.3 13.5 %all-gather.1 = f32[1,64,256]{1,2,0:T(8,128)S(1)} all-gather(f32[1,64,64]{1,2,0:T(8,128)S(1)} %copy.27), channel_id=3, replica_groups=mesh['row'=8,'col'=4] {'col'}, dimensions={2}, use_global_device_ids=true | all-gather | bytes 81920 | tf_op jit(solution)/shard_map/all_gather | solution.py:21
  47.9 0.3 convolution_bitcast_fusion.4
  48.2 0.1 copy.21
  48.2 9.3 %all_gather.21 = f32[512,128]{1,0:T(8,128)S(1)} all-gather(f32[64,128]{1,0:T(8,128)S(1)} %copy.21), channel_id=1, replica_groups=mesh['row'=8,'col'=4] {'row'}, dimensions={0}, use_global_device_ids=true | all-gather | bytes 294912 | tf_op jit(solution)/shard_map/all_gather | solution.py:31
  57.5 1.1 convolution_bitcast_fusion.1
  58.6 0.0 reduce-scatter.6.cloned.1.call-update
  58.6 0.0 reduce-scatter.8.cloned.1.call-start
  58.6 0.1 copy.28
  58.7 13.7 %all-gather.2 = f32[1,64,256]{1,2,0:T(8,128)S(1)} all-gather(f32[1,64,64]{1,2,0:T(8,128)S(1)} %copy.28), channel_id=4, replica_groups=mesh['row'=8,'col'=4] {'col'}, dimensions={2}, use_global_device_ids=true | all-gather | bytes 81920 | tf_op jit(solution)/shard_map/all_gather | solution.py:21
  72.4 0.3 convolution_bitcast_fusion.3
  72.7 0.1 copy.25
  72.8 8.7 %all_gather.23 = f32[512,128]{1,0:T(8,128)S(1)} all-gather(f32[64,128]{1,0:T(8,128)S(1)} %copy.25), channel_id=1, replica_groups=mesh['row'=8,'col'=4] {'row'}, dimensions={0}, use_global_device_ids=true | all-gather | bytes 294912 | tf_op jit(solution)/shard_map/all_gather | solution.py:31
  81.5 1.1 convolution_bitcast_fusion
  82.6 0.0 reduce-scatter.8.cloned.1.call-update
  82.6 0.0 reduce-scatter.4.cloned.1.call-done
  82.7 0.8 negate_bitcast_fusion
  83.4 0.0 reduce-scatter.6.cloned.1.call-done
  83.4 0.0 copy-done.1
  83.4 1.4 %fusion.2 = f32[16,512]{1,0:T(8,128)S(1)} fusion(f32[16,512]{1,0:T(8,128)} %reduce-scatter.6.cloned.1.call-done, f32[2,512,512]{2,1,0:T(8,128)S(1)} %copy-done.1, f32[16,512]{1,0:T(8,128)} %reduce-scatter.4.cloned.1.call-done), kind=kOutput, calls=%fused_computation.10 | convolution fusion | flops 50356224 | bytes 1146880 | tf_op jit(solution)/shard_map/dot_general | solution.py:38
  84.8 18.2 %reduce-scatter.8.cloned.1.call-done = f32[16,512]{1,0:T(8,128)} async-done(((f32[64,512]{1,0:T(8,128)}), f32[16,512]{1,0:T(8,128)}) %reduce-scatter.8.cloned.1.call-update) | async-done | bytes 32784 | tf_op jit(solution)/shard_map/reduce_scatter | solution.py:36
  103.0 1.4 %fusion.1 = f32[1,16,512]{2,1,0:T(8,128)S(1)} fusion(f32[16,512]{1,0:T(8,128)} %reduce-scatter.8.cloned.1.call-done, f32[16,512]{1,0:T(8,128)S(1)} %fusion.2, f32[2,512,512]{2,1,0:T(8,128)S(1)} %copy-done.1), kind=kOutput, calls=%fused_computation.8 | convolution fusion | flops 50348032 | bytes 1146880 | tf_op jit(solution)/shard_map/dot_general | solution.py:38
  104.4 0.6 pad_maximum_fusion
  (4 shorter events, 0.0 us)
Async XLA Ops:
  6.5 26.6 %copy-start = (f32[64,128]{1,0:T(8,128)S(1)}, f32[64,128]{1,0:T(8,128)}, u32[]{:S(2)}) copy-start(f32[64,128]{1,0:T(8,128)} %param.4) | copy-start | bytes 98308
  6.5 76.1 %reduce-scatter.4.cloned.1.call-start = ((), (), s32[]{:S(2)}) async-start(), calls=%async_computation.3 | async-start | bytes 163840 | tf_op jit(solution)/shard_map/reduce_scatter | solution.py:36
  23.6 59.9 %copy-start.1 = (f32[2,512,512]{2,1,0:T(8,128)S(1)}, f32[2,512,512]{2,1,0:T(8,128)}, u32[]{:S(2)}) copy-start(f32[2,512,512]{2,1,0:T(8,128)} %param.7) | copy-start | bytes 6291460
  34.2 49.2 %reduce-scatter.6.cloned.1.call-start = ((), (), s32[]{:S(2)}) async-start(), calls=%async_computation.4 | async-start | bytes 163840 | tf_op jit(solution)/shard_map/reduce_scatter | solution.py:36
  58.6 44.4 %reduce-scatter.8.cloned.1.call-start = ((), (), s32[]{:S(2)}) async-start(), calls=%async_computation.5 | async-start | bytes 163840 | tf_op jit(solution)/shard_map/reduce_scatter | solution.py:36
Sparse Core Ops, SparseCore 0:
  34.3 19.9 reduce-scatter.3
  58.7 20.2 reduce-scatter.5
  82.8 20.2 reduce-scatter.7
where the time goes:
time: 112 us
  blocking collectives  69.8 us (62%)
  waiting for transfers between devices  18.3 us (16%)
  between operations  13.2 us (12%)
  matrix products  6.76 us (6%)
  local copies, waits for them, and re-layouts  2.04 us (2%)
  other arithmetic  1.41 us (1%)
    all_gather x3, blocking collectives, on_device(): gathered = lax.all_gather(factor_panels[section], 'col', axis=1, tiled=True)  42.3 us
    all_gather x3, blocking collectives, on_device(): lax.all_gather(picked, 'row', axis=0, tiled=True)  27.5 us
    reduce_scatter x3, waiting for transfers between devices, on_device(): lax.psum_scatter(partial_value, 'col', scatter_dimension=0, tiled=True)  18.2 us
    dot_general x3, matrix products, on_device(): lax.dot_general(inverse_tiles, lax.all_gather(picked, 'row', axis=0, tile...  3.21 us
    dot_general x2, matrix products, on_device(): jnp.dot(previous, couplings[section - 1], precision=lax.Precision.HIGHEST...  2.76 us
  transfers between devices with their start and end apart: 3, of which 1 were waited for; matrix products, arithmetic and copies ran while one was open for 5% of the time, Pallas kernels for 0%

commit v1 on v0

--- a/solution.py
+++ b/solution.py
@@ -18,7 +18,14 @@
     previous = None
     for section in range(factor_panels.shape[0]):
         section_rows = block_rows[section]
-        gathered = lax.all_gather(factor_panels[section], "col", axis=1, tiled=True)
+        ring = [factor_panels[section]]
+        for hop in range(3):
+            ring.append(lax.ppermute(ring[-1], "col", [(dev, (dev + 1) % 4) for dev in range(4)]))
+        gathered = jnp.roll(
+            jnp.concatenate(ring[::-1], axis=1),
+            (lax.axis_index("col") + 1) * ring[0].shape[1],
+            axis=1,
+        )
         onehot = (section_rows[:, None] == targets[None, :]).astype(jnp.float32)
         picked = jnp.einsum(
             "wpr,pq->wqr",

time: 112 us -> 104 us (0.929)
  blocking collectives: 69.8 us -> 27.5 us
  waiting for transfers between devices: 18.3 us -> 45.1 us
  starting transfers between devices: 0.09 us -> 6.95 us
    all_gather x3 -> x0, blocking collectives: 42.3 us -> none  [on_device(): gathered = lax.all_gather(factor_panels[section], 'col', axis=1, tiled=True)]
    reduce_scatter x3, waiting for transfers between devices: 18.2 us -> 34.3 us  [on_device(): lax.psum_scatter(partial_value, 'col', scatter_dimension=0, tiled=True)]
    ppermute x0 -> x9, waiting for transfers between devices: none -> 10.8 us  [on_device(): lax.ppermute(ring[-1], 'col', [(dev, (dev + 1) % 4) for dev in range(4)])]
    ppermute x0 -> x9, starting transfers between devices: none -> 6.87 us  [on_device(): lax.ppermute(ring[-1], 'col', [(dev, (dev + 1) % 4) for dev in range(4)])]
  transfers between devices with their start and end apart: 3 -> 12, of which waited for: 1 -> 9; matrix products, arithmetic and copies ran while one was open for 5% -> 8% of each run, Pallas kernels for 0% -> 0%
where the time goes in v1:
time: 104 us
  waiting for transfers between devices  45.1 us (43%)
  blocking collectives  27.5 us (26%)
  between operations  13.2 us (13%)
  starting transfers between devices  6.95 us (7%)
  matrix products  6.81 us (7%)
  other arithmetic  2.08 us (2%)
  local copies, waits for them, and re-layouts  2.04 us (2%)
    reduce_scatter x3, waiting for transfers between devices, on_device(): lax.psum_scatter(partial_value, 'col', scatter_dimension=0, tiled=True)  34.3 us
    all_gather x3, blocking collectives, on_device(): lax.all_gather(picked, 'row', axis=0, tiled=True)  27.5 us
    ppermute x9, waiting for transfers between devices, on_device(): lax.ppermute(ring[-1], 'col', [(dev, (dev + 1) % 4) for dev in range(4)])  10.8 us
    ppermute x9, starting transfers between devices, on_device(): lax.ppermute(ring[-1], 'col', [(dev, (dev + 1) % 4) for dev in range(4)])  6.87 us
    dot_general x3, matrix products, on_device(): lax.dot_general(inverse_tiles, lax.all_gather(picked, 'row', axis=0, tile...  3.23 us
    dot_general x2, matrix products, on_device(): jnp.dot(previous, couplings[section - 1], precision=lax.Precision.HIGHEST...  2.76 us
  transfers between devices with their start and end apart: 12, of which 9 were waited for; matrix products, arithmetic and copies ran while one was open for 8% of the time, Pallas kernels for 0%

profile of v1, /device:TPU:0, one launch (start us, length us, event | category | flops | bytes accessed | tf_op | source)
XLA Modules:
  0.0 103.7 jit_solution(17755596409267579146)
XLA Ops:
  6.5 0.0 copy-start
  6.5 0.0 reduce-scatter.4.cloned.1.call-start
  6.5 0.8 fusion.44
  7.3 0.1 copy.26
  7.4 3.1 %collective-permute-start = (f32[64,64]{0,1:T(8,128)S(1)}, f32[64,64]{0,1:T(8,128)S(1)}, u32[]{:S(2)}, u32[]{:S(2)}) collective-permute-start(f32[64,64]{0,1:T(8,128)S(1)} %bitcast.65), channel_id=1, source_target_pairs={{0,1},{1,2},{2,3},{3,0},{4,5},{5,6},{6,7},{7,4},{8,9},{9,10},{10,1... | collective-permute-start | bytes 49160 | tf_op jit(solution)/shard_map/ppermute | solution.py:23
  10.5 0.1 copy.27
  10.6 1.6 %collective-permute-start.3 = (f32[64,64]{0,1:T(8,128)S(1)}, f32[64,64]{0,1:T(8,128)S(1)}, u32[]{:S(2)}, u32[]{:S(2)}) collective-permute-start(f32[64,64]{0,1:T(8,128)S(1)} %bitcast.61), channel_id=1, source_target_pairs={{0,1},{1,2},{2,3},{3,0},{4,5},{5,6},{6,7},{7,4},{8,9},{9,10},{10,1... | collective-permute-start | bytes 49160 | tf_op jit(solution)/shard_map/ppermute | solution.py:23
  12.2 0.1 copy.28
  12.2 1.6 %collective-permute-start.6 = (f32[64,64]{0,1:T(8,128)S(1)}, f32[64,64]{0,1:T(8,128)S(1)}, u32[]{:S(2)}, u32[]{:S(2)}) collective-permute-start(f32[64,64]{0,1:T(8,128)S(1)} %bitcast.63), channel_id=1, source_target_pairs={{0,1},{1,2},{2,3},{3,0},{4,5},{5,6},{6,7},{7,4},{8,9},{9,10},{10,1... | collective-permute-start | bytes 49160 | tf_op jit(solution)/shard_map/ppermute | solution.py:23
  13.9 0.6 collective-permute-done
  14.4 0.1 collective-permute-start.1
  14.5 0.8 slice_bitcast_fusion.2
  15.3 1.3 %collective-permute-done.3 = f32[64,64]{0,1:T(8,128)S(1)} collective-permute-done((f32[64,64]{0,1:T(8,128)S(1)}, f32[64,64]{0,1:T(8,128)S(1)}, u32[]{:S(2)}, u32[]{:S(2)}) %collective-permute-start.3) | collective-permute-done | bytes 16416 | tf_op jit(solution)/shard_map/ppermute | solution.py:23
  16.6 0.2 collective-permute-start.4
  16.9 1.3 %collective-permute-done.6 = f32[64,64]{0,1:T(8,128)S(1)} collective-permute-done((f32[64,64]{0,1:T(8,128)S(1)}, f32[64,64]{0,1:T(8,128)S(1)}, u32[]{:S(2)}, u32[]{:S(2)}) %collective-permute-start.6) | collective-permute-done | bytes 16416 | tf_op jit(solution)/shard_map/ppermute | solution.py:23
  18.2 0.2 collective-permute-start.7
  18.4 1.7 %collective-permute-done.1 = f32[64,64]{0,1:T(8,128)S(1)} collective-permute-done((f32[64,64]{0,1:T(8,128)S(1)}, f32[64,64]{0,1:T(8,128)S(1)}, u32[]{:S(2)}, u32[]{:S(2)}) %collective-permute-start.1) | collective-permute-done | bytes 16416 | tf_op jit(solution)/shard_map/ppermute | solution.py:23
  20.1 0.0 collective-permute-start.2
  20.2 2.2 %collective-permute-done.4 = f32[64,64]{0,1:T(8,128)S(1)} collective-permute-done((f32[64,64]{0,1:T(8,128)S(1)}, f32[64,64]{0,1:T(8,128)S(1)}, u32[]{:S(2)}, u32[]{:S(2)}) %collective-permute-start.4) | collective-permute-done | bytes 16416 | tf_op jit(solution)/shard_map/ppermute | solution.py:23
  22.4 0.0 collective-permute-start.5
  22.4 1.8 %collective-permute-done.7 = f32[64,64]{0,1:T(8,128)S(1)} collective-permute-done((f32[64,64]{0,1:T(8,128)S(1)}, f32[64,64]{0,1:T(8,128)S(1)}, u32[]{:S(2)}, u32[]{:S(2)}) %collective-permute-start.7) | collective-permute-done | bytes 16416 | tf_op jit(solution)/shard_map/ppermute | solution.py:23
  24.1 0.0 collective-permute-start.8
  24.1 1.8 %collective-permute-done.2 = f32[64,64]{0,1:T(8,128)S(1)} collective-permute-done((f32[64,64]{0,1:T(8,128)S(1)}, f32[64,64]{0,1:T(8,128)S(1)}, u32[]{:S(2)}, u32[]{:S(2)}) %collective-permute-start.2) | collective-permute-done | bytes 16416 | tf_op jit(solution)/shard_map/ppermute | solution.py:23
  26.0 0.3 fusion.24
  26.3 0.3 convolution_bitcast_fusion.5
  26.6 0.0 copy-start.1
  26.6 0.1 copy.17
  26.7 9.8 %all_gather.9 = f32[512,128]{1,0:T(8,128)S(1)} all-gather(f32[64,128]{1,0:T(8,128)S(1)} %copy.17), channel_id=1, replica_groups=mesh['row'=8,'col'=4] {'row'}, dimensions={0}, use_global_device_ids=true | all-gather | bytes 294912 | tf_op jit(solution)/shard_map/all_gather | solution.py:38
  36.5 0.0 copy-done
  36.5 1.1 %convolution_bitcast_fusion.2 = f32[64,512]{1,0:T(8,128)} fusion(f32[512,128]{1,0:T(8,128)S(1)} %all_gather.9, f32[64,128]{1,0:T(8,128)S(1)} %copy-done), kind=kOutput, calls=%fused_computation.2 | convolution fusion | flops 50331648 | bytes 425984 | tf_op jit(solution)/shard_map/dot_general | solution.py:36
  37.6 0.0 reduce-scatter.4.cloned.1.call-update
  37.6 0.0 reduce-scatter.6.cloned.1.call-start
  37.7 0.0 collective-permute-done.5
  37.7 0.0 collective-permute-done.8
  37.7 0.3 fusion.10
  38.0 0.3 convolution_bitcast_fusion.4
  38.3 0.1 copy.21
  38.4 0.3 convolution_bitcast_fusion.3
  38.7 9.3 %all_gather.10 = f32[512,128]{1,0:T(8,128)S(1)} all-gather(f32[64,128]{1,0:T(8,128)S(1)} %copy.21), channel_id=1, replica_groups=mesh['row'=8,'col'=4] {'row'}, dimensions={0}, use_global_device_ids=true | all-gather | bytes 294912 | tf_op jit(solution)/shard_map/all_gather | solution.py:38
  48.0 0.1 copy.25
  48.0 1.1 %convolution_bitcast_fusion.1 = f32[64,512]{1,0:T(8,128)} fusion(f32[512,128]{1,0:T(8,128)S(1)} %all_gather.10, f32[64,128]{1,0:T(8,128)S(1)} %copy-done), kind=kOutput, calls=%fused_computation.1 | convolution fusion | flops 50331648 | bytes 425984 | tf_op jit(solution)/shard_map/dot_general | solution.py:36
  49.1 0.0 reduce-scatter.6.cloned.1.call-update
  49.2 0.0 reduce-scatter.8.cloned.1.call-start
  49.2 8.3 %all_gather.11 = f32[512,128]{1,0:T(8,128)S(1)} all-gather(f32[64,128]{1,0:T(8,128)S(1)} %copy.25), channel_id=1, replica_groups=mesh['row'=8,'col'=4] {'row'}, dimensions={0}, use_global_device_ids=true | all-gather | bytes 294912 | tf_op jit(solution)/shard_map/all_gather | solution.py:38
  57.5 1.1 %convolution_bitcast_fusion = f32[64,512]{1,0:T(8,128)} fusion(f32[512,128]{1,0:T(8,128)S(1)} %all_gather.11, f32[64,128]{1,0:T(8,128)S(1)} %copy-done), kind=kOutput, calls=%fused_computation | convolution fusion | flops 50331648 | bytes 425984 | tf_op jit(solution)/shard_map/dot_general | solution.py:36
  58.6 0.0 reduce-scatter.8.cloned.1.call-update
  58.6 0.0 reduce-scatter.4.cloned.1.call-done
  58.7 0.8 negate_bitcast_fusion
  59.4 15.8 %reduce-scatter.6.cloned.1.call-done = f32[16,512]{1,0:T(8,128)} async-done(((f32[64,512]{1,0:T(8,128)}), f32[16,512]{1,0:T(8,128)}) %reduce-scatter.6.cloned.1.call-update) | async-done | bytes 32784 | tf_op jit(solution)/shard_map/reduce_scatter | solution.py:43
  75.3 0.0 copy-done.1
  75.3 1.4 %fusion.2 = f32[16,512]{1,0:T(8,128)S(1)} fusion(f32[16,512]{1,0:T(8,128)} %reduce-scatter.6.cloned.1.call-done, f32[2,512,512]{2,1,0:T(8,128)S(1)} %copy-done.1, f32[16,512]{1,0:T(8,128)} %reduce-scatter.4.cloned.1.call-done), kind=kOutput, calls=%fused_computation.10 | convolution fusion | flops 50356224 | bytes 1146880 | tf_op jit(solution)/shard_map/dot_general | solution.py:45
  76.6 18.5 %reduce-scatter.8.cloned.1.call-done = f32[16,512]{1,0:T(8,128)} async-done(((f32[64,512]{1,0:T(8,128)}), f32[16,512]{1,0:T(8,128)}) %reduce-scatter.8.cloned.1.call-update) | async-done | bytes 32784 | tf_op jit(solution)/shard_map/reduce_scatter | solution.py:43
  95.1 1.4 %fusion.1 = f32[1,16,512]{2,1,0:T(8,128)S(1)} fusion(f32[16,512]{1,0:T(8,128)} %reduce-scatter.8.cloned.1.call-done, f32[16,512]{1,0:T(8,128)S(1)} %fusion.2, f32[2,512,512]{2,1,0:T(8,128)S(1)} %copy-done.1), kind=kOutput, calls=%fused_computation.8 | convolution fusion | flops 50348032 | bytes 1146880 | tf_op jit(solution)/shard_map/dot_general | solution.py:45
  96.5 0.6 pad_maximum_fusion
  (4 shorter events, 0.0 us)
Async XLA Ops:
  6.5 30.0 %copy-start = (f32[64,128]{1,0:T(8,128)S(1)}, f32[64,128]{1,0:T(8,128)}, u32[]{:S(2)}) copy-start(f32[64,128]{1,0:T(8,128)} %param.6) | copy-start | bytes 98308
  6.5 52.1 %reduce-scatter.4.cloned.1.call-start = ((), (), s32[]{:S(2)}) async-start(), calls=%async_computation.3 | async-start | bytes 163840 | tf_op jit(solution)/shard_map/reduce_scatter | solution.py:43
  7.4 7.0 %collective-permute-start = (f32[64,64]{0,1:T(8,128)S(1)}, f32[64,64]{0,1:T(8,128)S(1)}, u32[]{:S(2)}, u32[]{:S(2)}) collective-permute-start(f32[64,64]{0,1:T(8,128)S(1)} %bitcast.65), channel_id=1, source_target_pairs={{0,1},{1,2},{2,3},{3,0},{4,5},{5,6},{6,7},{7,4},{8,9},{9,10},{10,1... | collective-permute-start | bytes 49160 | tf_op jit(solution)/shard_map/ppermute | solution.py:23
  10.6 6.1 %collective-permute-start.3 = (f32[64,64]{0,1:T(8,128)S(1)}, f32[64,64]{0,1:T(8,128)S(1)}, u32[]{:S(2)}, u32[]{:S(2)}) collective-permute-start(f32[64,64]{0,1:T(8,128)S(1)} %bitcast.61), channel_id=1, source_target_pairs={{0,1},{1,2},{2,3},{3,0},{4,5},{5,6},{6,7},{7,4},{8,9},{9,10},{10,1... | collective-permute-start | bytes 49160 | tf_op jit(solution)/shard_map/ppermute | solution.py:23
  12.2 5.9 %collective-permute-start.6 = (f32[64,64]{0,1:T(8,128)S(1)}, f32[64,64]{0,1:T(8,128)S(1)}, u32[]{:S(2)}, u32[]{:S(2)}) collective-permute-start(f32[64,64]{0,1:T(8,128)S(1)} %bitcast.63), channel_id=1, source_target_pairs={{0,1},{1,2},{2,3},{3,0},{4,5},{5,6},{6,7},{7,4},{8,9},{9,10},{10,1... | collective-permute-start | bytes 49160 | tf_op jit(solution)/shard_map/ppermute | solution.py:23
  14.4 5.7 %collective-permute-start.1 = (f32[64,64]{0,1:T(8,128)S(1)}, f32[64,64]{0,1:T(8,128)S(1)}, u32[]{:S(2)}, u32[]{:S(2)}) collective-permute-start(f32[64,64]{0,1:T(8,128)S(1)} %collective-permute-done), channel_id=1, source_target_pairs={{0,1},{1,2},{2,3},{3,0},{4,5},{5,6},{6,7},{7,4},{8,9},{9,10},{10,1... | collective-permute-start | bytes 49160 | tf_op jit(solution)/shard_map/ppermute | solution.py:23
  16.6 5.7 %collective-permute-start.4 = (f32[64,64]{0,1:T(8,128)S(1)}, f32[64,64]{0,1:T(8,128)S(1)}, u32[]{:S(2)}, u32[]{:S(2)}) collective-permute-start(f32[64,64]{0,1:T(8,128)S(1)} %collective-permute-done.3), channel_id=1, source_target_pairs={{0,1},{1,2},{2,3},{3,0},{4,5},{5,6},{6,7},{7,4},{8,9},{9,10},{10,1... | collective-permute-start | bytes 49160 | tf_op jit(solution)/shard_map/ppermute | solution.py:23
  18.2 5.9 %collective-permute-start.7 = (f32[64,64]{0,1:T(8,128)S(1)}, f32[64,64]{0,1:T(8,128)S(1)}, u32[]{:S(2)}, u32[]{:S(2)}) collective-permute-start(f32[64,64]{0,1:T(8,128)S(1)} %collective-permute-done.6), channel_id=1, source_target_pairs={{0,1},{1,2},{2,3},{3,0},{4,5},{5,6},{6,7},{7,4},{8,9},{9,10},{10,1... | collective-permute-start | bytes 49160 | tf_op jit(solution)/shard_map/ppermute | solution.py:23
  20.1 5.9 %collective-permute-start.2 = (f32[64,64]{0,1:T(8,128)S(1)}, f32[64,64]{0,1:T(8,128)S(1)}, u32[]{:S(2)}, u32[]{:S(2)}) collective-permute-start(f32[64,64]{0,1:T(8,128)S(1)} %collective-permute-done.1), channel_id=1, source_target_pairs={{0,1},{1,2},{2,3},{3,0},{4,5},{5,6},{6,7},{7,4},{8,9},{9,10},{10,1... | collective-permute-start | bytes 49160 | tf_op jit(solution)/shard_map/ppermute | solution.py:23
  22.4 15.3 %collective-permute-start.5 = (f32[64,64]{0,1:T(8,128)S(1)}, f32[64,64]{0,1:T(8,128)S(1)}, u32[]{:S(2)}, u32[]{:S(2)}) collective-permute-start(f32[64,64]{0,1:T(8,128)S(1)} %collective-permute-done.4), channel_id=1, source_target_pairs={{0,1},{1,2},{2,3},{3,0},{4,5},{5,6},{6,7},{7,4},{8,9},{9,10},{10,1... | collective-permute-start | bytes 49160 | tf_op jit(solution)/shard_map/ppermute | solution.py:23
  24.1 13.5 %collective-permute-start.8 = (f32[64,64]{0,1:T(8,128)S(1)}, f32[64,64]{0,1:T(8,128)S(1)}, u32[]{:S(2)}, u32[]{:S(2)}) collective-permute-start(f32[64,64]{0,1:T(8,128)S(1)} %collective-permute-done.7), channel_id=1, source_target_pairs={{0,1},{1,2},{2,3},{3,0},{4,5},{5,6},{6,7},{7,4},{8,9},{9,10},{10,1... | collective-permute-start | bytes 49160 | tf_op jit(solution)/shard_map/ppermute | solution.py:23
  26.6 48.7 %copy-start.1 = (f32[2,512,512]{2,1,0:T(8,128)S(1)}, f32[2,512,512]{2,1,0:T(8,128)}, u32[]{:S(2)}) copy-start(f32[2,512,512]{2,1,0:T(8,128)} %param.9) | copy-start | bytes 6291460
  37.6 37.6 %reduce-scatter.6.cloned.1.call-start = ((), (), s32[]{:S(2)}) async-start(), calls=%async_computation.4 | async-start | bytes 163840 | tf_op jit(solution)/shard_map/reduce_scatter | solution.py:43
  49.2 46.0 %reduce-scatter.8.cloned.1.call-start = ((), (), s32[]{:S(2)}) async-start(), calls=%async_computation.5 | async-start | bytes 163840 | tf_op jit(solution)/shard_map/reduce_scatter | solution.py:43
Sparse Core Ops, SparseCore 0:
  37.7 17.6 reduce-scatter.3
  57.7 17.5 reduce-scatter.5
  77.5 17.5 reduce-scatter.7
